TPU v7x, 512 devices: a whole 4x4x16 slice. The times are simulated.
512 devices in a mesh: phase: 4 (over x), dp: 16 (over z), mp: 8 (over y, core).
Axes of the slice: x: 4, y: 4, z: 16, core: 2. Of those that a mesh axis runs over, the one named last changes fastest.
Arguments:
- text_rows: bfloat16 [2048, 4096], P('dp', 'mp'), may hold values from -6 to 6
- image_rows: bfloat16 [32, 128, 1280], P('dp', ('phase', 'mp')), may hold values from -6 to 6
- tile_counts: int32 [32], P('dp'), may hold values from 1 to 4
- text_lengths: int32 [32], P('dp'), may hold values from 1 to 64
- sample_image: int32 [32], P('dp'), may hold values from 0 to 1
- norm_gain: float32 [4, 4096], P('phase'), may hold values from 0.5 to 2
- query_weight: bfloat16 [4, 4096, 4096], P('phase', 'dp', 'mp'), may hold values from -0.09375 to 0.09375
- keyval_weight: bfloat16 [4, 1280, 8, 256], P('phase', None, 'mp'), may hold values from -0.15625 to 0.15625
- output_weight: bfloat16 [4, 4096, 4096], P('phase', 'dp', 'mp'), may hold values from -0.09375 to 0.09375
- cross_gate: float32 [4], P('phase'), may hold values from -1.5 to 1.5
Outputs:
- section_states: bfloat16 [4, 2048, 4096], P('phase', 'dp', 'mp')
All inputs are finite; a program needn't handle non-finite values.
Results may differ from a plain program's by a relative error of at most 0.014.
Values may be sent and summed in bfloat16 or wider, within the bound.
A program may use at most 64 MiB of HBM per device.

v0:
```python
import jax
import jax.numpy as jnp
from jax import lax
from jax.sharding import PartitionSpec as P

HD = 128
HQ_DEV = 4
TROWS = 32
SAMP = 2
TXT = 64


epsilon = 1e-05


def from_behind(block, axis, distance):
    devices = range(lax.axis_size(axis))
    route = [(i - distance, i) for i in devices if i - distance in devices]
    return lax.ppermute(block, axis, route)


def on_device(
    text_rows,
    image_rows,
    tile_counts,
    text_lengths,
    sample_image,
    norm_gain,
    query_weight,
    keyval_weight,
    output_weight,
    cross_gate,
):
    phases = lax.axis_size("phase")
    phase_index = lax.axis_index("phase")
    mp_index = lax.axis_index("mp")
    wq_full, wo_full = (
        lax.all_gather(query_weight[0], "dp", axis=0, tiled=True),
        lax.all_gather(output_weight[0], "dp", axis=0, tiled=True),
    )
    kv_local = keyval_weight[0, :, 0, :]
    keyval = jnp.einsum(
        "srv,vc->src",
        lax.all_gather(image_rows, ("phase", "mp"), axis=1, tiled=True),
        kv_local,
        preferred_element_type=jnp.float32,
    ).astype(jnp.bfloat16)
    key_count = keyval.shape[1]
    keyval = keyval.reshape(SAMP * key_count, 2 * HD)
    key_rows = keyval[:, :HD]
    value_rows = keyval[:, HD:]
    own_rows = text_rows.shape[0]
    slice_width = text_rows.shape[1]
    key_index = jnp.arange(SAMP * key_count, dtype=jnp.int32)
    key_image = key_index // key_count
    image_pick = (key_image[:, None] == jnp.arange(SAMP, dtype=jnp.int32)[None, :]).astype(
        jnp.int32
    )
    key_valid = key_index % key_count < jnp.sum(image_pick * tile_counts[None, :], axis=1) * TROWS
    row_index = jnp.arange(own_rows, dtype=jnp.int32)
    row_pick = ((row_index // TXT)[:, None] == jnp.arange(SAMP, dtype=jnp.int32)[None, :]).astype(
        jnp.int32
    )
    row_image = jnp.sum(row_pick * sample_image[None, :], axis=1)
    row_length = jnp.sum(row_pick * text_lengths[None, :], axis=1)
    live = (row_index % TXT < row_length).astype(jnp.float32)
    allowed = ((row_image[:, None] == key_image[None, :]) & key_valid[None, :]).astype(jnp.float32)
    gate_value = jnp.tanh(cross_gate[0])
    gain_row = norm_gain[0]
    scale = float(HD) ** (-0.5)
    result = jnp.zeros_like(text_rows)

    def spread(own_part):
        return lax.all_gather(own_part, "mp", axis=1, tiled=True)

    full_rows = spread(text_rows)
    for turn_index in range(phases):
        own_slice = lax.dynamic_slice_in_dim(full_rows, mp_index * slice_width, slice_width, 1)
        row_count = full_rows.shape[0]
        widened = full_rows.astype(jnp.float32)
        mean_square = jnp.mean(widened * widened, axis=-1, keepdims=True)
        normed = (widened * lax.rsqrt(mean_square + epsilon) * gain_row).astype(jnp.bfloat16)
        queries = jnp.dot(normed, wq_full, preferred_element_type=jnp.float32).astype(jnp.bfloat16)
        queries = queries.reshape(row_count, HQ_DEV, HD)
        scores = (
            jnp.einsum("rhd,kd->hrk", queries, key_rows, preferred_element_type=jnp.float32) * scale
        )
        weighted = jnp.exp(scores) * allowed[None]
        weights = (weighted / jnp.sum(weighted, axis=-1, keepdims=True)).astype(jnp.bfloat16)
        context_rows = jnp.einsum(
            "hrk,kd->rhd", weights, value_rows, preferred_element_type=jnp.float32
        ).astype(jnp.bfloat16)
        context_rows = context_rows.reshape(row_count, HQ_DEV * HD)
        attended = jnp.dot(
            lax.all_gather(context_rows, "mp", axis=1, tiled=True),
            wo_full,
            preferred_element_type=jnp.float32,
        )
        updated = (own_slice.astype(jnp.float32) + live[:, None] * gate_value * attended).astype(
            jnp.bfloat16
        )
        result = jnp.where(phase_index == turn_index, updated, result)
        if turn_index + 1 < phases:
            full_rows = from_behind(spread(updated), "phase", 1)
    return result[None]


def solution(mesh):
    placed = (
        P("dp", "mp"),
        P("dp", ("phase", "mp"), None),
        P("dp"),
        P("dp"),
        P("dp"),
        P("phase", None),
        P("phase", "dp", "mp"),
        P("phase", None, "mp", None),
        P("phase", "dp", "mp"),
        P("phase"),
    )
    return jax.shard_map(
        on_device, mesh=mesh, in_specs=placed, out_specs=P("phase", "dp", "mp"), check_vma=False
    )
```

profile of v0, /device:TPU:7, one launch (start us, length us, event | category | flops | bytes accessed | tf_op | source)
XLA Modules:
  0.0 538.1 jit_solution(1307083336937461031)
XLA Ops:
  8.8 0.7 copy.37
  10.3 0.8 select_reduce_fusion.1
  11.1 28.2 %all_gather.34 = bf16[2,128,1280]{2,0,1:T(2,128)(2,1)S(1)} all-gather(bf16[2,4,1280]{2,0,1:T(2,128)(2,1)S(1)} %copy.37), channel_id=1, replica_groups=mesh['phase'=4,'dp'=16,'mp'=8] {'phase','mp'}, dimensions={1}, use_global_device_ids=true | all-gather | bytes 675840 | tf_op jit(solution)/shard_map/all_gather | solution.py:44
  39.7 5.7 %all-gather.13.cloned.1.call-done = bf16[128,4096]{1,0:T(8,128)(2,1)} async-done(((bf16[128,512]{1,0:T(8,128)(2,1)}), bf16[128,4096]{1,0:T(8,128)(2,1)}) %all-gather.13.cloned.1.call-update) | async-done | bytes 1048592 | tf_op jit(solution)/shard_map/all_gather | solution.py:74
  45.4 1.5 fusion.16
  46.9 70.0 %all-gather.29.cloned.1.call-done = bf16[1,4096,512]{2,1,0:T(8,128)(2,1)} async-done(((bf16[1,256,512]{2,1,0:T(8,128)(2,1)}), bf16[1,4096,512]{2,1,0:T(8,128)(2,1)}) %all-gather.29.cloned.1.call-update) | async-done | bytes 4194320 | tf_op jit(solution)/shard_map/all_gather | solution.py:38
  117.0 3.3 fusion.79
  120.5 0.9 convolution_convert_fusion.3
  122.2 72.2 %all-gather.31.cloned.1.call-done = bf16[1,4096,512]{2,1,0:T(8,128)(2,1)} async-done(((bf16[1,256,512]{2,1,0:T(8,128)(2,1)}), bf16[1,4096,512]{2,1,0:T(8,128)(2,1)}) %all-gather.31.cloned.1.call-update) | async-done | bytes 4194320 | tf_op jit(solution)/shard_map/all_gather | solution.py:39
  194.3 38.9 %all-gather.15.cloned.1.call-done = bf16[128,4096]{0,1:T(8,128)(2,1)} async-done(((bf16[128,512]{0,1:T(8,128)(2,1)}), bf16[128,4096]{0,1:T(8,128)(2,1)}) %all-gather.15.cloned.1.call-update) | async-done | bytes 1048592 | tf_op jit(solution)/shard_map/all_gather | solution.py:95
  233.2 3.9 fusion.67
  237.2 31.1 %all-gather.17.cloned.1.call-done = bf16[128,4096]{1,0:T(8,128)(2,1)} async-done(((bf16[128,512]{1,0:T(8,128)(2,1)}), bf16[128,4096]{1,0:T(8,128)(2,1)}) %all-gather.17.cloned.1.call-update) | async-done | bytes 1048592 | tf_op jit(solution)/shard_map/all_gather | solution.py:74
  268.3 1.3 collective-permute-start
  269.6 25.3 %collective-permute-done = bf16[128,4096]{1,0:T(8,128)(2,1)S(1)} collective-permute-done((bf16[128,4096]{1,0:T(8,128)(2,1)}, bf16[128,4096]{1,0:T(8,128)(2,1)S(1)}, u32[]{:S(2)}, u32[]{:S(2)}) %collective-permute-start) | collective-permute-done | bytes 1048608 | tf_op jit(solution)/shard_map/ppermute | solution.py:19
  295.2 3.0 fusion.76
  298.4 0.9 convolution_convert_fusion.2
  299.4 31.9 %all-gather.19.cloned.1.call-done = bf16[128,4096]{0,1:T(8,128)(2,1)} async-done(((bf16[128,512]{0,1:T(8,128)(2,1)}), bf16[128,4096]{0,1:T(8,128)(2,1)}) %all-gather.19.cloned.1.call-update) | async-done | bytes 1048592 | tf_op jit(solution)/shard_map/all_gather | solution.py:95
  331.3 3.9 add_convert_fusion.2
  335.3 31.1 %all-gather.21.cloned.1.call-done = bf16[128,4096]{1,0:T(8,128)(2,1)} async-done(((bf16[128,512]{1,0:T(8,128)(2,1)}), bf16[128,4096]{1,0:T(8,128)(2,1)}) %all-gather.21.cloned.1.call-update) | async-done | bytes 1048592 | tf_op jit(solution)/shard_map/all_gather | solution.py:74
  366.3 1.3 collective-permute-start.1
  367.6 25.3 %collective-permute-done.1 = bf16[128,4096]{1,0:T(8,128)(2,1)S(1)} collective-permute-done((bf16[128,4096]{1,0:T(8,128)(2,1)}, bf16[128,4096]{1,0:T(8,128)(2,1)S(1)}, u32[]{:S(2)}, u32[]{:S(2)}) %collective-permute-start.1) | collective-permute-done | bytes 1048608 | tf_op jit(solution)/shard_map/ppermute | solution.py:19
  393.2 3.0 fusion.73
  396.5 0.9 convolution_convert_fusion.1
  397.4 31.9 %all-gather.23.cloned.1.call-done = bf16[128,4096]{0,1:T(8,128)(2,1)} async-done(((bf16[128,512]{0,1:T(8,128)(2,1)}), bf16[128,4096]{0,1:T(8,128)(2,1)}) %all-gather.23.cloned.1.call-update) | async-done | bytes 1048592 | tf_op jit(solution)/shard_map/all_gather | solution.py:95
  429.3 3.9 add_convert_fusion.1
  433.3 31.1 %all-gather.25.cloned.1.call-done = bf16[128,4096]{1,0:T(8,128)(2,1)} async-done(((bf16[128,512]{1,0:T(8,128)(2,1)}), bf16[128,4096]{1,0:T(8,128)(2,1)}) %all-gather.25.cloned.1.call-update) | async-done | bytes 1048592 | tf_op jit(solution)/shard_map/all_gather | solution.py:74
  464.4 1.3 collective-permute-start.2
  465.7 25.3 %collective-permute-done.2 = bf16[128,4096]{1,0:T(8,128)(2,1)S(1)} collective-permute-done((bf16[128,4096]{1,0:T(8,128)(2,1)}, bf16[128,4096]{1,0:T(8,128)(2,1)S(1)}, u32[]{:S(2)}, u32[]{:S(2)}) %collective-permute-start.2) | collective-permute-done | bytes 1048608 | tf_op jit(solution)/shard_map/ppermute | solution.py:19
  491.3 3.0 fusion.70
  494.5 0.9 convolution_convert_fusion
  495.5 31.9 %all-gather.27.cloned.1.call-done = bf16[128,4096]{0,1:T(8,128)(2,1)} async-done(((bf16[128,512]{0,1:T(8,128)(2,1)}), bf16[128,4096]{0,1:T(8,128)(2,1)}) %all-gather.27.cloned.1.call-update) | async-done | bytes 1048592 | tf_op jit(solution)/shard_map/all_gather | solution.py:95
  527.4 3.9 fusion.101
  (48 shorter events, 5.7 us)
Async XLA Ops:
  6.5 32.8 %copy-start = (bf16[1,1280,1,256]{3,1,2,0:T(8,128)(2,1)S(1)}, bf16[1,1280,1,256]{3,1,2,0:T(8,128)(2,1)}, u32[]{:S(2)}) copy-start(bf16[1,1280,1,256]{3,1,2,0:T(8,128)(2,1)} %param.17) | copy-start | bytes 1966084
  6.5 110.4 %copy-start.4 = (f32[1,4096]{1,0:T(1,128)S(1)}, f32[1,4096]{1,0:T(1,128)}, u32[]{:S(2)}) copy-start(f32[1,4096]{1,0:T(1,128)} %param.15) | copy-start | bytes 49156
  6.5 38.9 %all-gather.13.cloned.1.call-start = ((), (), s32[]{:S(2)}) async-start(), calls=%async_computation | async-start | bytes 1179648 | tf_op jit(solution)/shard_map/all_gather | solution.py:74
  7.3 109.7 %all-gather.29.cloned.1.call-start = ((), (), s32[]{:S(2)}) async-start(), calls=%async_computation.8 | async-start | bytes 4456448 | tf_op jit(solution)/shard_map/all_gather | solution.py:38
  8.0 186.3 %all-gather.31.cloned.1.call-start = ((), (), s32[]{:S(2)}) async-start(), calls=%async_computation.9 | async-start | bytes 4456448 | tf_op jit(solution)/shard_map/all_gather | solution.py:39
  8.7 224.5 %all-gather.15.cloned.1.call-start = ((), (), s32[]{:S(2)}) async-start(), calls=%async_computation.1 | async-start | bytes 1179648 | tf_op jit(solution)/shard_map/all_gather | solution.py:95
  121.4 146.9 %all-gather.17.cloned.1.call-start = ((), (), s32[]{:S(2)}) async-start(), calls=%async_computation.2 | async-start | bytes 1179648 | tf_op jit(solution)/shard_map/all_gather | solution.py:74
  237.1 94.1 %all-gather.19.cloned.1.call-start = ((), (), s32[]{:S(2)}) async-start(), calls=%async_computation.3 | async-start | bytes 1179648 | tf_op jit(solution)/shard_map/all_gather | solution.py:95
  268.3 26.6 %collective-permute-start = (bf16[128,4096]{1,0:T(8,128)(2,1)}, bf16[128,4096]{1,0:T(8,128)(2,1)S(1)}, u32[]{:S(2)}, u32[]{:S(2)}) collective-permute-start(bf16[128,4096]{1,0:T(8,128)(2,1)} %all-gather.17.cloned.1.call-done), channel_id=1, source_target_pairs={{0,128},{128,256},{256,384},{1,129},{129,257},{257,385},{2,130},{1... | collective-permute-start | bytes 3145736 | tf_op jit(solution)/shard_map/ppermute | solution.py:19
  299.4 67.0 %all-gather.21.cloned.1.call-start = ((), (), s32[]{:S(2)}) async-start(), calls=%async_computation.4 | async-start | bytes 1179648 | tf_op jit(solution)/shard_map/all_gather | solution.py:74
  335.2 94.1 %all-gather.23.cloned.1.call-start = ((), (), s32[]{:S(2)}) async-start(), calls=%async_computation.5 | async-start | bytes 1179648 | tf_op jit(solution)/shard_map/all_gather | solution.py:95
  366.3 26.6 %collective-permute-start.1 = (bf16[128,4096]{1,0:T(8,128)(2,1)}, bf16[128,4096]{1,0:T(8,128)(2,1)S(1)}, u32[]{:S(2)}, u32[]{:S(2)}) collective-permute-start(bf16[128,4096]{1,0:T(8,128)(2,1)} %all-gather.21.cloned.1.call-done), channel_id=1, source_target_pairs={{0,128},{128,256},{256,384},{1,129},{129,257},{257,385},{2,130},{1... | collective-permute-start | bytes 3145736 | tf_op jit(solution)/shard_map/ppermute | solution.py:19
  397.4 67.0 %all-gather.25.cloned.1.call-start = ((), (), s32[]{:S(2)}) async-start(), calls=%async_computation.6 | async-start | bytes 1179648 | tf_op jit(solution)/shard_map/all_gather | solution.py:74
  433.2 94.1 %all-gather.27.cloned.1.call-start = ((), (), s32[]{:S(2)}) async-start(), calls=%async_computation.7 | async-start | bytes 1179648 | tf_op jit(solution)/shard_map/all_gather | solution.py:95
  464.4 26.6 %collective-permute-start.2 = (bf16[128,4096]{1,0:T(8,128)(2,1)}, bf16[128,4096]{1,0:T(8,128)(2,1)S(1)}, u32[]{:S(2)}, u32[]{:S(2)}) collective-permute-start(bf16[128,4096]{1,0:T(8,128)(2,1)} %all-gather.25.cloned.1.call-done), channel_id=1, source_target_pairs={{0,128},{128,256},{256,384},{1,129},{129,257},{257,385},{2,130},{1... | collective-permute-start | bytes 3145736 | tf_op jit(solution)/shard_map/ppermute | solution.py:19
  494.2 33.1 %copy-start.1 = (bf16[128,512]{1,0:T(8,128)(2,1)S(1)}, bf16[128,512]{1,0:T(8,128)(2,1)}, u32[]{:S(2)}) copy-start(bf16[128,512]{1,0:T(8,128)(2,1)} %fusion.67) | copy-start | bytes 393220
  494.3 33.1 %copy-start.2 = (bf16[128,512]{1,0:T(8,128)(2,1)S(1)}, bf16[128,512]{1,0:T(8,128)(2,1)}, u32[]{:S(2)}) copy-start(bf16[128,512]{1,0:T(8,128)(2,1)} %add_convert_fusion.2) | copy-start | bytes 393220
  494.3 33.1 %copy-start.3 = (bf16[128,512]{1,0:T(8,128)(2,1)S(1)}, bf16[128,512]{1,0:T(8,128)(2,1)}, u32[]{:S(2)}) copy-start(bf16[128,512]{1,0:T(8,128)(2,1)} %add_convert_fusion.1) | copy-start | bytes 393220
Sparse Core Ops, SparseCore 0:
  9.5 35.8 all-gather.12
  47.5 69.4 all-gather.28
  119.0 75.2 all-gather.30
  196.4 36.8 all-gather.14
  237.3 30.9 all-gather.16
  299.5 31.7 all-gather.18
  335.3 30.9 all-gather.20
  397.5 31.7 all-gather.22
  433.4 30.9 all-gather.24
  495.6 31.7 all-gather.26
where the time goes:
time: 540 us; the launch traced here: 538 us
  waiting for transfers between devices  454 us (84%)
  matrix products  32.7 us (6%)
  blocking collectives  28.2 us (5%)
  between operations  14.4 us (3%)
    all_gather x4, waiting for transfers between devices, on_device(): lax.all_gather(context_rows, 'mp', axis=1, tiled=True)  135 us
    all_gather x4, waiting for transfers between devices, spread(): return lax.all_gather(own_part, 'mp', axis=1, tiled=True)  99 us
    ppermute x3, waiting for transfers between devices, from_behind(): return lax.ppermute(block, axis, route)  76 us
    all_gather x1, waiting for transfers between devices, on_device(): lax.all_gather(output_weight[0], 'dp', axis=0, tiled=True)  72.2 us
    all_gather x1, waiting for transfers between devices, on_device(): lax.all_gather(query_weight[0], 'dp', axis=0, tiled=True)  70 us
    all_gather x1, blocking collectives, on_device(): lax.all_gather(image_rows, ('phase', 'mp'), axis=1, tiled=True)  28.2 us
    dot_general x4, matrix products, on_device(): jnp.dot(lax.all_gather(context_rows, 'mp', axis=1, tiled=True), wo_full,...  15.7 us
    dot_general x4, matrix products, on_device(): jnp.dot(normed, wq_full, preferred_element_type=jnp.float32)  12.1 us
  transfers between devices with their start and end apart: 13, of which 13 were waited for; matrix products, arithmetic and copies ran while one was open for 2% of the time, Pallas kernels for 0%

commit v1 on v0

v1 whole, which is shorter than its diff:
```python
import functools

import jax
import jax.numpy as jnp
from jax import lax
from jax.experimental import pallas as pl
from jax.experimental.pallas import tpu as pltpu
from jax.sharding import PartitionSpec as P

MESH = pl.DeviceIdType.MESH
HD = 128
TROWS = 32
SAMP = 2
SUBS = 2
PARTS = 9

epsilon = 1e-05


def kernel(
    sizes,
    tiles_ref,
    lengths_ref,
    pick_ref,
    gate_ref,
    x_in,
    image_in,
    gain_ref,
    wq_in,
    wkv_ref,
    wo_in,
    out_ref,
    wq_buf,
    wo_buf,
    x_buf,
    ctx_buf,
    image_buf,
    kv_buf,
    acc,
    local_sem,
    ring_send,
    ring_recv,
    spread_send,
    spread_recv,
    image_send,
    image_recv,
    hop_send,
    hop_recv,
):
    phases, ring, groups = sizes
    phase = lax.axis_index("phase")
    d = lax.axis_index("dp")
    m = lax.axis_index("mp")
    rows, width = x_in.shape
    half_rows = rows // SAMP
    depth = wq_in.shape[0]
    sub = depth // SUBS
    steps = ring // 2
    first = phase == 0

    up, down = lax.rem(d + 1, ring), lax.rem(d + ring - 1, ring)
    sibling = m + 1 - 2 * lax.rem(m, 2)
    right, left = lax.rem(m + 2, groups), lax.rem(m + groups - 2, groups)
    across = lax.rem(m + 4, groups)

    def twin(slot):
        return slot + 1 - 2 * lax.rem(slot, 2)

    own_wq = pltpu.make_async_copy(
        wq_in, wq_buf.at[pl.ds(pl.multiple_of(d * depth, depth), depth), :], local_sem.at[0]
    )
    own_wo = pltpu.make_async_copy(
        wo_in, wo_buf.at[pl.ds(pl.multiple_of(d * depth, depth), depth), :], local_sem.at[1]
    )
    piece = image_in.shape[0]
    place = phase * groups + m
    own_image = pltpu.make_async_copy(
        image_in, image_buf.at[pl.ds(pl.multiple_of(place * piece, piece), piece), :], local_sem.at[2]
    )
    own_x = pltpu.make_async_copy(x_in, x_buf.at[m], local_sem.at[3])
    own_wq.start()
    own_wo.start()
    own_image.start()

    @pl.when(first)
    def _():
        own_x.start()

    barrier = pltpu.get_barrier_semaphore()
    for target in (up, down):
        pl.semaphore_signal(barrier, inc=1, device_id={"dp": target}, device_id_type=MESH)
    for k in range(1, groups):
        pl.semaphore_signal(
            barrier, inc=1, device_id={"mp": lax.rem(m + k, groups)}, device_id_type=MESH
        )
    for k in range(1, phases):
        pl.semaphore_signal(
            barrier, inc=1, device_id={"phase": lax.rem(phase + k, phases)}, device_id_type=MESH
        )
    own_wq.wait()
    own_wo.wait()
    own_image.wait()

    @pl.when(first)
    def _():
        own_x.wait()

    pl.semaphore_wait(barrier, 2 + groups - 1 + phases - 1)

    def ring_copy(mat, s, u, way, incoming=False):
        shift = s + 1 if incoming else s
        block = lax.rem(d + (ring - shift if way == 0 else shift), ring)
        at = pl.ds(pl.multiple_of(block * depth + u * sub, sub), sub)
        buf = (wq_buf, wo_buf)[mat].at[at, :]
        index = (((mat * 2 + way) * steps) + s) * SUBS + u
        return pltpu.make_async_remote_copy(
            src_ref=buf,
            dst_ref=buf,
            send_sem=ring_send.at[index],
            recv_sem=ring_recv.at[index],
            device_id={"dp": up if way == 0 else down},
            device_id_type=MESH,
        )

    def used(s, u, way):
        return s < steps - 1 or (u < SUBS // 2) == (way == 0)

    def ring_step(mat, s):
        for u in range(SUBS):
            for way in range(2):
                if used(s, u, way):
                    if s > 0:
                        ring_copy(mat, s - 1, u, way, True).wait_recv()
                    ring_copy(mat, s, u, way).start()

    def ring_end(mat):
        for u in range(SUBS):
            for way in range(2):
                last = steps - 1 if used(steps - 1, u, way) else steps - 2
                ring_copy(mat, last, u, way, True).wait_recv()

    def ring_sent(mat):
        for s in range(steps):
            for u in range(SUBS):
                for way in range(2):
                    if used(s, u, way):
                        ring_copy(mat, s, u, way).wait_send()

    def image_copy(k, incoming=False):
        owner = lax.rem(m + groups - k, groups) if incoming else m
        at = pl.ds(pl.multiple_of((phase * groups + owner) * piece, piece), piece)
        return pltpu.make_async_remote_copy(
            src_ref=image_buf.at[at, :],
            dst_ref=image_buf.at[at, :],
            send_sem=image_send.at[k],
            recv_sem=image_recv.at[k],
            device_id={"mp": lax.rem(m + k, groups)},
            device_id_type=MESH,
        )

    def image_block_copy(k, incoming=False):
        owner = lax.rem(phase + phases - k, phases) if incoming else phase
        span = groups * piece
        at = pl.ds(pl.multiple_of(owner * span, span), span)
        return pltpu.make_async_remote_copy(
            src_ref=image_buf.at[at, :],
            dst_ref=image_buf.at[at, :],
            send_sem=image_send.at[groups + k],
            recv_sem=image_recv.at[groups + k],
            device_id={"phase": lax.rem(phase + k, phases)},
            device_id_type=MESH,
        )

    def spread_copy(which, h, part, incoming=False):
        buf = (x_buf, ctx_buf)[which]
        start, count = h * half_rows, half_rows
        quarter = half_rows // 2
        target = sibling
        if part == 0:
            slot = sibling if incoming else m
        elif part == 1:
            slot, target = (left if incoming else m), right
        elif part == 2:
            slot, target = (right if incoming else m), left
        elif part == 3:
            slot = twin(left) if incoming else left
        elif part == 4:
            slot = twin(right) if incoming else right
        elif part == 5:
            slot, target, count = (across if incoming else left), right, quarter
        elif part == 6:
            slot, target, count = (across if incoming else right), left, quarter
            start += quarter
        elif part == 7:
            slot, count = (twin(across) if incoming else across), quarter
        else:
            slot, count = (twin(across) if incoming else across), quarter
            start += quarter
        ref = buf.at[slot, pl.ds(start, count), :]
        index = (which * SAMP + h) * PARTS + part
        return pltpu.make_async_remote_copy(
            src_ref=ref,
            dst_ref=ref,
            send_sem=spread_send.at[index],
            recv_sem=spread_recv.at[index],
            device_id={"mp": target},
            device_id_type=MESH,
        )

    def spread_open(which, h):
        for part in (1, 2, 0):
            spread_copy(which, h, part).start()

    def spread_pass(which, h):
        spread_copy(which, h, 1, True).wait_recv()
        spread_copy(which, h, 5).start()
        spread_copy(which, h, 3).start()
        spread_copy(which, h, 2, True).wait_recv()
        spread_copy(which, h, 6).start()
        spread_copy(which, h, 4).start()

    def spread_far(which, h):
        for part in (5, 6):
            spread_copy(which, h, part, True).wait_recv()
            spread_copy(which, h, part + 2).start()

    def spread_sent(which, h):
        for part in range(PARTS):
            spread_copy(which, h, part).wait_send()

    def hop_copy(h):
        at = pl.ds(h * half_rows, half_rows)
        return pltpu.make_async_remote_copy(
            src_ref=out_ref.at[at, :],
            dst_ref=x_buf.at[m, at, :],
            send_sem=hop_send.at[h],
            recv_sem=hop_recv.at[h],
            device_id={"phase": lax.rem(phase + 1, phases)},
            device_id_type=MESH,
        )

    def make_keyval():
        kv_buf[...] = jnp.dot(
            image_buf[...], wkv_ref[...], preferred_element_type=jnp.float32
        ).astype(jnp.bfloat16)

    def column(slot):
        return pl.ds(pl.multiple_of(slot * width, width), width)

    def query_term(h, slot, squares, begin=False):
        at = pl.ds(h * half_rows, half_rows)
        wide = x_buf[slot, at, :].astype(jnp.float32)
        scaled = (wide * gain_ref[:, column(slot)]).astype(jnp.bfloat16)
        term = jnp.dot(scaled, wq_buf[column(slot), :], preferred_element_type=jnp.float32)
        if begin:
            acc[at, :] = term
        else:
            acc[at, :] += term
        part = jnp.sum(wide * wide, axis=-1, keepdims=True)
        return part if squares is None else squares + part

    def attend(h, squares):
        at = pl.ds(h * half_rows, half_rows)
        factor = lax.rsqrt(squares / (width * groups) + epsilon)
        queries = (acc[at, :] * factor).astype(jnp.bfloat16)
        count = kv_buf.shape[0]
        key = lax.broadcasted_iota(jnp.int32, (half_rows, count), 1)
        per = piece // SAMP
        image = (key // per) % SAMP
        row = (key // piece) * per + key % per
        limit = jnp.where(image == 0, tiles_ref[0], tiles_ref[1]) * TROWS
        allowed = ((row < limit) & (image == pick_ref[h])).astype(jnp.float32)
        for g in range(width // HD):
            cols = slice(g * HD, (g + 1) * HD)
            scores = lax.dot_general(
                queries[:, cols],
                kv_buf[:, :HD],
                (((1,), (1,)), ((), ())),
                preferred_element_type=jnp.float32,
            ) * (float(HD) ** (-0.5))
            prob = jnp.exp(scores) * allowed
            weights = (prob / jnp.sum(prob, axis=-1, keepdims=True)).astype(jnp.bfloat16)
            ctx_buf[m, at, cols] = jnp.dot(
                weights, kv_buf[:, HD:], preferred_element_type=jnp.float32
            ).astype(jnp.bfloat16)

    def out_term(h, slot, begin=False):
        at = pl.ds(h * half_rows, half_rows)
        term = jnp.dot(
            ctx_buf[slot, at, :], wo_buf[column(slot), :], preferred_element_type=jnp.float32
        )
        if begin:
            acc[at, :] = term
        else:
            acc[at, :] += term

    def finish(h):
        at = pl.ds(h * half_rows, half_rows)
        position = lax.broadcasted_iota(jnp.int32, (half_rows, width), 0)
        gate = jnp.tanh(jnp.full((half_rows, width), gate_ref[0], jnp.float32))
        moved = jnp.where(position < lengths_ref[h], gate * acc[at, :], 0.0)
        out_ref[at, :] = (x_buf[m, at, :].astype(jnp.float32) + moved).astype(jnp.bfloat16)

        @pl.when(phase < phases - 1)
        def _():
            hop_copy(h).start()

    def query_rest(h, squares):
        spread_copy(0, h, 0, True).wait_recv()
        squares = query_term(h, sibling, squares)
        squares = query_term(h, left, squares)
        squares = query_term(h, right, squares)
        spread_copy(0, h, 3, True).wait_recv()
        squares = query_term(h, twin(left), squares)
        spread_copy(0, h, 4, True).wait_recv()
        squares = query_term(h, twin(right), squares)
        squares = query_term(h, across, squares)
        for part in (7, 8):
            spread_copy(0, h, part, True).wait_recv()
        return query_term(h, twin(across), squares)

    def out_rest(h):
        spread_copy(1, h, 0, True).wait_recv()
        out_term(h, sibling)
        out_term(h, left)
        out_term(h, right)
        spread_copy(1, h, 3, True).wait_recv()
        out_term(h, twin(left))
        spread_copy(1, h, 4, True).wait_recv()
        out_term(h, twin(right))
        out_term(h, across)
        for part in (7, 8):
            spread_copy(1, h, part, True).wait_recv()
        out_term(h, twin(across))

    halves = range(SAMP)

    ring_step(0, 0)
    for k in range(1, groups):
        image_copy(k).start()

    @pl.when(first)
    def _():
        for h in halves:
            spread_open(0, h)

    for k in range(1, groups):
        image_copy(k, True).wait_recv()
    for k in range(1, phases):
        image_block_copy(k).start()

    @pl.when(first)
    def _():
        for h in halves:
            spread_pass(0, h)

    ring_step(0, 1)

    @pl.when(first)
    def _():
        for h in halves:
            spread_far(0, h)

    ring_step(0, 2)
    ring_step(0, 3)
    for k in range(1, phases):
        image_block_copy(k, True).wait_recv()
    make_keyval()
    for s in range(4, steps):
        ring_step(0, s)
    ring_step(1, 0)
    ring_end(0)

    @pl.when(first)
    def _():
        for h in halves:
            attend(h, query_rest(h, query_term(h, m, None, True)))
            spread_open(1, h)

    ring_step(1, 1)

    @pl.when(first)
    def _():
        for h in halves:
            spread_pass(1, h)

    ring_step(1, 2)
    ring_step(1, 3)

    @pl.when(first)
    def _():
        for h in halves:
            spread_far(1, h)

    for s in range(4, steps):
        ring_step(1, s)
    ring_end(1)

    @pl.when(first)
    def _():
        for h in halves:
            out_term(h, m, True)
            out_rest(h)
            finish(h)

    @pl.when(phase > 0)
    def _():
        for h in halves:
            hop_copy(h).wait_recv()
            spread_open(0, h)
        for h in halves:
            squares = query_term(h, m, None, True)
            spread_pass(0, h)
            spread_far(0, h)
            attend(h, query_rest(h, squares))
            spread_open(1, h)
        for h in halves:
            out_term(h, m, True)
            spread_pass(1, h)
            spread_far(1, h)
            out_rest(h)
            finish(h)

    for mat in range(2):
        ring_sent(mat)
    for k in range(1, groups):
        image_copy(k).wait_send()
    for k in range(1, phases):
        image_block_copy(k).wait_send()
    for which in range(2):
        for h in halves:
            spread_sent(which, h)

    @pl.when(phase < phases - 1)
    def _():
        for h in halves:
            hop_copy(h).wait_send()


def solution(mesh):
    sizes = (mesh.shape["phase"], mesh.shape["dp"], mesh.shape["mp"])
    phases, ring, groups = sizes

    def on_device(
        text_rows,
        image_rows,
        tile_counts,
        text_lengths,
        sample_image,
        norm_gain,
        query_weight,
        keyval_weight,
        output_weight,
        cross_gate,
    ):
        rows, width = text_rows.shape
        samples, piece, vision = image_rows.shape
        depth = query_weight.shape[1]
        columns = query_weight.shape[2]
        smem = pl.BlockSpec(memory_space=pltpu.SMEM)
        vmem = pl.BlockSpec(memory_space=pltpu.VMEM)
        anywhere = pl.BlockSpec(memory_space=pl.ANY)
        keys = samples * piece * phases * groups
        ring_copies = 2 * 2 * (ring // 2) * SUBS
        result = pl.pallas_call(
            functools.partial(kernel, sizes),
            out_shape=jax.ShapeDtypeStruct((rows, width), jnp.bfloat16),
            in_specs=[smem] * 4 + [anywhere, anywhere, vmem, anywhere, vmem, anywhere],
            out_specs=vmem,
            scratch_shapes=[
                pltpu.VMEM((ring * depth, columns), jnp.bfloat16),
                pltpu.VMEM((ring * depth, columns), jnp.bfloat16),
                pltpu.VMEM((groups, rows, width), jnp.bfloat16),
                pltpu.VMEM((groups, rows, width), jnp.bfloat16),
                pltpu.VMEM((keys, vision), jnp.bfloat16),
                pltpu.VMEM((keys, 2 * HD), jnp.bfloat16),
                pltpu.VMEM((rows, width), jnp.float32),
                pltpu.SemaphoreType.DMA((4,)),
                pltpu.SemaphoreType.DMA((ring_copies,)),
                pltpu.SemaphoreType.DMA((ring_copies,)),
                pltpu.SemaphoreType.DMA((2 * SAMP * PARTS,)),
                pltpu.SemaphoreType.DMA((2 * SAMP * PARTS,)),
                pltpu.SemaphoreType.DMA((groups + phases,)),
                pltpu.SemaphoreType.DMA((groups + phases,)),
                pltpu.SemaphoreType.DMA((SAMP,)),
                pltpu.SemaphoreType.DMA((SAMP,)),
            ],
            compiler_params=pltpu.CompilerParams(
                collective_id=0, has_side_effects=True, vmem_limit_bytes=40 * 1024 * 1024
            ),
        )(
            tile_counts,
            text_lengths,
            sample_image,
            cross_gate,
            text_rows,
            image_rows.reshape(samples * piece, vision),
            norm_gain,
            query_weight[0],
            keyval_weight[0, :, 0, :],
            output_weight[0],
        )
        return result[None]

    placed = (
        P("dp", "mp"),
        P("dp", ("phase", "mp"), None),
        P("dp"),
        P("dp"),
        P("dp"),
        P("phase", None),
        P("phase", "dp", "mp"),
        P("phase", None, "mp", None),
        P("phase", "dp", "mp"),
        P("phase"),
    )
    return jax.shard_map(
        on_device, mesh=mesh, in_specs=placed, out_specs=P("phase", "dp", "mp"), check_vma=False
    )
```

time: 540 us -> 199 us (0.37)
  waiting for transfers between devices: 454 us -> 0 us
  Pallas kernels: 0 us -> 193 us
  matrix products: 32.7 us -> 0 us
  blocking collectives: 28.2 us -> 0 us
  between operations: 14.4 us -> 0.73 us
    all_gather x10 -> x0, waiting for transfers between devices: 376 us -> none  [the longest x4 135 us: on_device(): lax.all_gather(context_rows, 'mp', axis=1, tiled=True)]
    pallas_call x0 -> x1, Pallas kernels: none -> 193 us  [on_device(): pl.pallas_call(functools.partial(kernel, sizes), out_shape=jax.ShapeDtype...]
    ppermute x3 -> x0, waiting for transfers between devices: 76 us -> none  [from_behind(): return lax.ppermute(block, axis, route)]
    dot_general x17 -> x0, matrix products: 32.7 us -> none  [the longest x4 15.7 us: on_device(): jnp.dot(lax.all_gather(context_rows, 'mp', axis=1, tiled=True), wo_full,...]
    all_gather x1 -> x0, blocking collectives: 28.2 us -> none  [on_device(): lax.all_gather(image_rows, ('phase', 'mp'), axis=1, tiled=True)]
  transfers between devices with their start and end apart: 13 -> 0, of which waited for: 13 -> 0; matrix products, arithmetic and copies ran while one was open for 2% -> 0% of each run, Pallas kernels for 0% -> 0%
where the time goes in v1:
time: 199 us
  Pallas kernels  193 us (97%)
  local copies, waits for them, and re-layouts  5.32 us (3%)
    pallas_call x1, Pallas kernels, on_device(): pl.pallas_call(functools.partial(kernel, sizes), out_shape=jax.ShapeDtype...  193 us
    unnamed x17, local copies, waits for them, and re-layouts  4.56 us

profile of v1, /device:TPU:7, one launch (start us, length us, event | category | flops | bytes accessed | tf_op | source)
XLA Modules:
  0.0 198.6 jit_solution(14215585848306108771)
XLA Ops:
  0.7 0.0 copy-start.4
  0.7 0.0 copy-start.5
  0.7 0.0 copy-start.6
  0.7 0.0 copy-start.7
  0.7 0.8 reshape.3.image_in
  1.5 0.0 copy-done.4
  1.5 0.0 copy-done.5
  1.5 0.0 copy-done.6
  1.5 0.0 copy-done.7
  1.5 0.0 copy-start
  1.5 1.1 copy-done
  2.6 0.0 copy-start.1
  2.6 0.9 copy-done.1
  3.5 0.0 copy-start.2
  3.5 0.9 copy-done.2
  4.5 0.0 copy-start.3
  4.5 0.9 copy-done.3
  5.4 192.5 %shard_map.100 = bf16[128,512]{1,0:T(8,128)(2,1)S(1)} custom-call(s32[2]{0:T(128)S(1)} %copy-done.5, s32[2]{0:T(128)S(1)} %copy-done.6, s32[2]{0:T(128)S(1)} %copy-done.7, f32[1]{0:T(128)S(6)} %copy.12.gate_ref, bf16[128,512]{1,0:T(8,128)(2,1)S(1)} %copy-done.3, bf16[8,1280]{1,0:T(8,128)(2,1)S(1)} %reshape.3.image_in, f32[1,4096]{1,0:T(1,128)S(1)} %copy-done.4, ...), custom_call_target="tpu_custom_call" | custom-call | tf_op jit(solution)/shard_map/pallas_call | solution.py:465
  197.9 0.7 copy.13
Async XLA Ops:
  0.7 0.8 copy-start.4
  0.7 0.8 copy-start.5
  0.7 0.8 copy-start.6
  0.7 0.8 copy-start.7
  1.5 1.1 copy-start
  2.6 0.9 copy-start.1
  3.5 0.9 copy-start.2
  4.5 0.9 copy-start.3

commit v2 on v0

v2 whole, which is shorter than its diff:
```python
import functools

import jax
import jax.numpy as jnp
from jax import lax
from jax.experimental import pallas as pl
from jax.experimental.pallas import tpu as pltpu
from jax.sharding import PartitionSpec as P

MESH = pl.DeviceIdType.MESH
HD = 128
TROWS = 32
SAMP = 2
SUBS = 4
CHIPS = 4

epsilon = 1e-05


def kernel(
    sizes,
    tiles_in,
    lengths_in,
    pick_in,
    gate_in,
    x_in,
    image_in,
    gain_in,
    wq_in,
    wkv_in,
    wo_in,
    out_ref,
    tiles_ref,
    lengths_ref,
    pick_ref,
    gate_ref,
    gain_ref,
    wkv_ref,
    wq_buf,
    wo_buf,
    guest_buf,
    x_buf,
    ctx_buf,
    image_buf,
    kv_buf,
    acc,
    local_sem,
    ring_send,
    ring_recv,
    guest_send,
    guest_recv,
    return_send,
    return_recv,
    cross_send,
    cross_recv,
    pair_send,
    pair_recv,
    image_send,
    image_recv,
):
    phases, ring, groups = sizes
    phase = lax.axis_index("phase")
    d = lax.axis_index("dp")
    m = lax.axis_index("mp")
    rows, width = x_in.shape
    half_rows = rows // SAMP
    depth = wq_in.shape[0]
    sub = depth // SUBS
    steps = ring // 2
    heads = width // HD

    up, down = lax.rem(d + 1, ring), lax.rem(d + ring - 1, ring)
    ahead = lax.rem(phase + 1, phases)
    behind = lax.rem(phase + phases - 1, phases)
    sibling = m + 1 - 2 * lax.rem(m, 2)

    def slot_of(j):
        return lax.rem(m + 2 * j, groups)

    def target_of(j):
        return lax.rem(m + groups - 2 * j, groups)

    def twin(slot):
        return slot + 1 - 2 * lax.rem(slot, 2)

    own_rows = pl.ds(pl.multiple_of(d * depth, depth), depth)
    piece = image_in.shape[0]
    place = pl.ds(pl.multiple_of((phase * groups + m) * piece, piece), piece)
    moves = (
        (wq_in, wq_buf.at[own_rows, :]),
        (image_in, image_buf.at[place, :]),
        (wo_in, wo_buf.at[own_rows, :]),
        (gain_in, gain_ref),
        (wkv_in, wkv_ref),
        (tiles_in, tiles_ref),
        (lengths_in, lengths_ref),
        (pick_in, pick_ref),
        (gate_in, gate_ref),
    )
    local = [
        pltpu.make_async_copy(source, target, local_sem.at[i])
        for i, (source, target) in enumerate(moves)
    ]
    for copy in local:
        copy.start()

    barrier = pltpu.get_barrier_semaphore()
    peers = [{"dp": up}, {"dp": down}]
    peers += [{"mp": lax.rem(m + k, groups)} for k in range(1, groups)]
    peers += [{"phase": lax.rem(phase + k, phases)} for k in range(1, phases)]
    peers += [{"phase": ahead, "mp": target_of(j)} for j in range(1, CHIPS)]
    peers += [{"phase": behind, "mp": slot_of(j)} for j in range(1, CHIPS)]
    for peer in peers:
        pl.semaphore_signal(barrier, inc=1, device_id=peer, device_id_type=MESH)
    for copy in local[:3]:
        copy.wait()
    pl.semaphore_wait(barrier, len(peers))

    def lane_on(mat, u):
        if mat == 0 or (mat == 1 and u < SUBS // 2):
            return None
        if mat == 1:
            return phase > (1 if u == SUBS - 1 else 0)
        if u < SUBS // 2:
            return False
        return phase >= (phases - 2 if u == SUBS - 1 else phases - 1)

    def guarded(predicate, move):
        if predicate is None:
            move()
        elif predicate is not False:
            pl.when(predicate)(move)

    def block_rows(s, u, way, incoming):
        shift = s + 1 if incoming else s
        block = lax.rem(d + (ring - shift if way == 0 else shift), ring)
        return pl.ds(pl.multiple_of(block * depth + u * sub, sub), sub)

    def ring_copy(mat, s, u, way, incoming=False):
        buf = (wq_buf, wo_buf, guest_buf)[mat].at[block_rows(s, u, way, incoming), :]
        index = ((mat * 2 + way) * steps + s) * SUBS + u
        return pltpu.make_async_remote_copy(
            src_ref=buf,
            dst_ref=buf,
            send_sem=ring_send.at[index],
            recv_sem=ring_recv.at[index],
            device_id={"dp": up if way == 0 else down},
            device_id_type=MESH,
        )

    mirror = phases - 1 - phase

    def guest_copy(u):
        at = pl.ds(pl.multiple_of(d * depth + u * sub, sub), sub)
        return pltpu.make_async_remote_copy(
            src_ref=wo_buf.at[at, :],
            dst_ref=guest_buf.at[at, :],
            send_sem=guest_send.at[u],
            recv_sem=guest_recv.at[u],
            device_id={"phase": mirror},
            device_id_type=MESH,
        )

    def return_copy(s, u, way):
        at = block_rows(s, u, way, True)
        index = (way * steps + s) * SUBS + u
        return pltpu.make_async_remote_copy(
            src_ref=guest_buf.at[at, :],
            dst_ref=wo_buf.at[at, :],
            send_sem=return_send.at[index],
            recv_sem=return_recv.at[index],
            device_id={"phase": mirror},
            device_id_type=MESH,
        )

    def goes_last(u, way):
        return u % 2 == way

    def ring_open(mat):
        for u in range(SUBS):

            def move(u=u):
                if mat == 2:
                    guest_copy(u).wait_recv()
                for way in range(2):
                    ring_copy(mat, 0, u, way).start()

            guarded(lane_on(mat, u), move)

    def ring_pass(mat, s, u, way, last):
        ring_copy(mat, s - 1, u, way, True).wait_recv()
        if not last:
            ring_copy(mat, s, u, way).start()
        if mat == 2:
            return_copy(s - 1, u, way).start()

    def ring_steps(mat, lo, hi):
        def one(s, carry):
            for u in range(SUBS):

                def move(u=u):
                    ring_pass(mat, s, u, u % 2, False)

                    @pl.when(s < steps - 1)
                    def _():
                        ring_pass(mat, s, u, 1 - u % 2, False)

                guarded(lane_on(mat, u), move)
            return carry

        lax.fori_loop(lo, hi, one, 0)

    def ring_end(mat):
        for u in range(SUBS):

            def move(u=u):
                for way in range(2):
                    ring_pass(mat, steps if goes_last(u, way) else steps - 1, u, way, True)

            guarded(lane_on(mat, u), move)

    def each_lane(predicate_of, act):
        def one(s, carry):
            for u in range(SUBS):

                def move(u=u):
                    act(s, u, u % 2)

                    @pl.when(s < steps - 1)
                    def _():
                        act(s, u, 1 - u % 2)

                guarded(predicate_of(u), move)
            return carry

        lax.fori_loop(0, steps, one, 0)

    def ring_sent(mat):
        each_lane(lambda u: lane_on(mat, u), lambda s, u, way: ring_copy(mat, s, u, way).wait_send())

    def hosted(u):
        if u < SUBS // 2:
            return False
        return phase < (2 if u == SUBS - 1 else 1)

    def image_copy(k, incoming=False):
        owner = lax.rem(m + groups - k, groups) if incoming else m
        at = pl.ds(pl.multiple_of((phase * groups + owner) * piece, piece), piece)
        return pltpu.make_async_remote_copy(
            src_ref=image_buf.at[at, :],
            dst_ref=image_buf.at[at, :],
            send_sem=image_send.at[k],
            recv_sem=image_recv.at[k],
            device_id={"mp": lax.rem(m + k, groups)},
            device_id_type=MESH,
        )

    def image_block_copy(k, incoming=False):
        owner = lax.rem(phase + phases - k, phases) if incoming else phase
        span = groups * piece
        at = pl.ds(pl.multiple_of(owner * span, span), span)
        return pltpu.make_async_remote_copy(
            src_ref=image_buf.at[at, :],
            dst_ref=image_buf.at[at, :],
            send_sem=image_send.at[groups + k],
            recv_sem=image_recv.at[groups + k],
            device_id={"phase": lax.rem(phase + k, phases)},
            device_id_type=MESH,
        )

    def cross_copy(which, h, j, source=None):
        at = pl.ds(h * half_rows, half_rows)
        index = (which * SAMP + h) * CHIPS + j
        target = {"mp": target_of(j)}
        if which == 0:
            target["phase"] = ahead
        dst = (x_buf, ctx_buf)[which].at[m, at, :]
        return pltpu.make_async_remote_copy(
            src_ref=dst if source is None else source.at[at, :],
            dst_ref=dst,
            send_sem=cross_send.at[index],
            recv_sem=cross_recv.at[index],
            device_id=target,
            device_id_type=MESH,
        )

    def pair_copy(which, h, j, incoming=False):
        slot = twin(slot_of(j)) if incoming else slot_of(j)
        ref = (x_buf, ctx_buf)[which].at[slot, pl.ds(h * half_rows, half_rows), :]
        index = (which * SAMP + h) * CHIPS + j
        return pltpu.make_async_remote_copy(
            src_ref=ref,
            dst_ref=ref,
            send_sem=pair_send.at[index],
            recv_sem=pair_recv.at[index],
            device_id={"mp": sibling},
            device_id_type=MESH,
        )

    def send_rows(h, source):
        for j in (2, 1, 3, 0):
            cross_copy(0, h, j, source).start()

    def make_keyval():
        kv_buf[...] = jnp.dot(
            image_buf[...], wkv_ref[...], preferred_element_type=jnp.float32
        ).astype(jnp.bfloat16)

    def column(slot):
        return pl.ds(pl.multiple_of(slot * width, width), width)

    def add(h, term, begin):
        at = pl.ds(h * half_rows, half_rows)
        if begin:
            acc[at, :] = term
        else:
            acc[at, :] += term

    def query_term(h, slot, squares, begin=False):
        wide = x_buf[slot, pl.ds(h * half_rows, half_rows), :].astype(jnp.float32)
        scaled = (wide * gain_ref[:, column(slot)]).astype(jnp.bfloat16)
        add(h, jnp.dot(scaled, wq_buf[column(slot), :], preferred_element_type=jnp.float32), begin)
        part = jnp.sum(wide * wide, axis=-1, keepdims=True)
        return part if begin else squares + part

    def out_term(h, slot, begin=False):
        rows_here = ctx_buf[slot, pl.ds(h * half_rows, half_rows), :]
        add(h, jnp.dot(rows_here, wo_buf[column(slot), :], preferred_element_type=jnp.float32), begin)

    def attend(h, squares):
        at = pl.ds(h * half_rows, half_rows)
        factor = lax.rsqrt(squares / (width * groups) + epsilon)
        queries = (acc[at, :] * factor).astype(jnp.bfloat16)
        stacked = jnp.concatenate([queries[:, g * HD : (g + 1) * HD] for g in range(heads)], axis=0)
        count = kv_buf.shape[0]
        key = lax.broadcasted_iota(jnp.int32, (1, count), 1)
        image = jnp.bitwise_and(jnp.right_shift(key, 2), 1)
        row = jnp.right_shift(key, 3) * 4 + jnp.bitwise_and(key, 3)
        limit = jnp.where(image == 0, tiles_ref[0], tiles_ref[1]) * TROWS
        allowed = ((row < limit) & (image == pick_ref[h])).astype(jnp.float32)
        scores = lax.dot_general(
            stacked, kv_buf[:, :HD], (((1,), (1,)), ((), ())), preferred_element_type=jnp.float32
        ) * (float(HD) ** (-0.5))
        prob = jnp.exp(scores) * allowed
        weights = (prob / jnp.sum(prob, axis=-1, keepdims=True)).astype(jnp.bfloat16)
        context = jnp.dot(weights, kv_buf[:, HD:], preferred_element_type=jnp.float32).astype(
            jnp.bfloat16
        )
        for g in range(heads):
            ctx_buf[m, at, g * HD : (g + 1) * HD] = context[g * half_rows : (g + 1) * half_rows, :]

    def section_front(h):
        squares = None
        for j in (0, 1, 3, 2):
            cross_copy(0, h, j).wait_recv()
            pair_copy(0, h, j).start()
            squares = query_term(h, slot_of(j), squares, begin=j == 0)
        for j in (0, 1, 3, 2):
            pair_copy(0, h, j, True).wait_recv()
            squares = query_term(h, twin(slot_of(j)), squares)
        attend(h, squares)
        for j in (2, 1, 3):
            cross_copy(1, h, j).start()
        pair_copy(1, h, 0).start()

    def section_back(h):
        out_term(h, m, True)
        for j in (1, 3, 2):
            cross_copy(1, h, j).wait_recv()
            pair_copy(1, h, j).start()
            out_term(h, slot_of(j))
        for j in (0, 1, 3, 2):
            pair_copy(1, h, j, True).wait_recv()
            out_term(h, twin(slot_of(j)))
        at = pl.ds(h * half_rows, half_rows)
        position = lax.broadcasted_iota(jnp.int32, (half_rows, width), 0)
        gate = jnp.tanh(jnp.full((1, width), gate_ref[0], jnp.float32))
        moved = jnp.where(position < lengths_ref[h], gate * acc[at, :], 0.0)
        out_ref[at, :] = (x_buf[m, at, :].astype(jnp.float32) + moved).astype(jnp.bfloat16)

        @pl.when(phase < phases - 1)
        def _():
            send_rows(h, out_ref)

    for u in range(SUBS):
        guarded(hosted(u), lambda u=u: guest_copy(u).start())
    ring_open(0)
    for k in range(1, groups):
        image_copy(k).start()

    @pl.when(phase == phases - 1)
    def _():
        for h in range(SAMP):
            send_rows(h, x_in)

    ring_open(2)
    for k in range(1, groups):
        image_copy(k, True).wait_recv()
    for k in range(1, phases):
        image_block_copy(k).start()
    middle = steps // 2
    for s in range(1, middle):
        ring_steps(2, 2 * s - 1, 2 * s)
        ring_steps(0, s, s + 1)
        ring_steps(2, 2 * s, 2 * s + 1)
    for k in range(1, phases):
        image_block_copy(k, True).wait_recv()
    for copy in local[3:]:
        copy.wait()
    make_keyval()
    ring_steps(2, steps - 1, steps)
    ring_steps(0, middle, middle + 1)
    ring_end(2)
    ring_open(1)
    for s in range(middle + 1, steps):
        ring_steps(0, s, s + 1)
        ring_steps(1, s - middle, s - middle + 1)
    ring_end(0)

    others = lax.div(phase + phases - 1, phases)
    pause = middle + (steps - middle) * others
    resume = pause + 1 - others
    ring_steps(1, middle, pause)
    section_front(0)
    ring_steps(1, pause, resume)
    section_front(1)
    ring_steps(1, resume, steps)
    ring_end(1)
    each_lane(hosted, lambda s, u, way: return_copy(s, u, way).wait_recv())
    for h in range(SAMP):
        section_back(h)

    for mat in range(3):
        ring_sent(mat)
    for u in range(SUBS):
        guarded(hosted(u), lambda u=u: guest_copy(u).wait_send())
    each_lane(lambda u: lane_on(2, u), lambda s, u, way: return_copy(s, u, way).wait_send())
    for k in range(1, groups):
        image_copy(k).wait_send()
    for k in range(1, phases):
        image_block_copy(k).wait_send()
    for h in range(SAMP):
        for j in range(CHIPS):
            cross_copy(0, h, j, out_ref).wait_send()
            pair_copy(0, h, j).wait_send()
            pair_copy(1, h, j).wait_send()
            if j:
                cross_copy(1, h, j).wait_send()


def solution(mesh):
    sizes = (mesh.shape["phase"], mesh.shape["dp"], mesh.shape["mp"])
    phases, ring, groups = sizes

    def on_device(
        text_rows,
        image_rows,
        tile_counts,
        text_lengths,
        sample_image,
        norm_gain,
        query_weight,
        keyval_weight,
        output_weight,
        cross_gate,
    ):
        rows, width = text_rows.shape
        samples, piece, vision = image_rows.shape
        depth = query_weight.shape[1]
        columns = query_weight.shape[2]
        vmem = pl.BlockSpec(memory_space=pltpu.VMEM)
        anywhere = pl.BlockSpec(memory_space=pl.ANY)
        keys = samples * piece * phases * groups
        lane_copies = 2 * (ring // 2) * SUBS
        result = pl.pallas_call(
            functools.partial(kernel, sizes),
            out_shape=jax.ShapeDtypeStruct((rows, width), jnp.bfloat16),
            in_specs=[anywhere] * 10,
            out_specs=vmem,
            scratch_shapes=[
                pltpu.SMEM(tile_counts.shape, jnp.int32),
                pltpu.SMEM(text_lengths.shape, jnp.int32),
                pltpu.SMEM(sample_image.shape, jnp.int32),
                pltpu.SMEM(cross_gate.shape, jnp.float32),
                pltpu.VMEM(norm_gain.shape, jnp.float32),
                pltpu.VMEM((vision, 2 * HD), jnp.bfloat16),
                pltpu.VMEM((ring * depth, columns), jnp.bfloat16),
                pltpu.VMEM((ring * depth, columns), jnp.bfloat16),
                pltpu.VMEM((ring * depth, columns), jnp.bfloat16),
                pltpu.VMEM((groups, rows, width), jnp.bfloat16),
                pltpu.VMEM((groups, rows, width), jnp.bfloat16),
                pltpu.VMEM((keys, vision), jnp.bfloat16),
                pltpu.VMEM((keys, 2 * HD), jnp.bfloat16),
                pltpu.VMEM((rows, width), jnp.float32),
                pltpu.SemaphoreType.DMA((9,)),
                pltpu.SemaphoreType.DMA((3 * lane_copies,)),
                pltpu.SemaphoreType.DMA((3 * lane_copies,)),
                pltpu.SemaphoreType.DMA((SUBS,)),
                pltpu.SemaphoreType.DMA((SUBS,)),
                pltpu.SemaphoreType.DMA((lane_copies,)),
                pltpu.SemaphoreType.DMA((lane_copies,)),
                pltpu.SemaphoreType.DMA((2 * SAMP * CHIPS,)),
                pltpu.SemaphoreType.DMA((2 * SAMP * CHIPS,)),
                pltpu.SemaphoreType.DMA((2 * SAMP * CHIPS,)),
                pltpu.SemaphoreType.DMA((2 * SAMP * CHIPS,)),
                pltpu.SemaphoreType.DMA((groups + phases,)),
                pltpu.SemaphoreType.DMA((groups + phases,)),
            ],
            compiler_params=pltpu.CompilerParams(
                collective_id=0, has_side_effects=True, vmem_limit_bytes=60 * 1024 * 1024
            ),
        )(
            tile_counts,
            text_lengths,
            sample_image,
            cross_gate,
            text_rows,
            image_rows.reshape(samples * piece, vision),
            norm_gain,
            query_weight[0],
            keyval_weight[0, :, 0, :],
            output_weight[0],
        )
        return result[None]

    placed = (
        P("dp", "mp"),
        P("dp", ("phase", "mp"), None),
        P("dp"),
        P("dp"),
        P("dp"),
        P("phase", None),
        P("phase", "dp", "mp"),
        P("phase", None, "mp", None),
        P("phase", "dp", "mp"),
        P("phase"),
    )
    return jax.shard_map(
        on_device, mesh=mesh, in_specs=placed, out_specs=P("phase", "dp", "mp"), check_vma=False
    )
```

time: 540 us -> 154 us (0.29)
  waiting for transfers between devices: 454 us -> 0 us
  Pallas kernels: 0 us -> 150 us
  matrix products: 32.7 us -> 0 us
  blocking collectives: 28.2 us -> 0 us
  between operations: 14.4 us -> 0.66 us
    all_gather x10 -> x0, waiting for transfers between devices: 376 us -> none  [the longest x4 135 us: on_device(): lax.all_gather(context_rows, 'mp', axis=1, tiled=True)]
    pallas_call x0 -> x1, Pallas kernels: none -> 150 us  [on_device(): pl.pallas_call(functools.partial(kernel, sizes), out_shape=jax.ShapeDtype...]
    ppermute x3 -> x0, waiting for transfers between devices: 76 us -> none  [from_behind(): return lax.ppermute(block, axis, route)]
    dot_general x17 -> x0, matrix products: 32.7 us -> none  [the longest x4 15.7 us: on_device(): jnp.dot(lax.all_gather(context_rows, 'mp', axis=1, tiled=True), wo_full,...]
    all_gather x1 -> x0, blocking collectives: 28.2 us -> none  [on_device(): lax.all_gather(image_rows, ('phase', 'mp'), axis=1, tiled=True)]
  transfers between devices with their start and end apart: 13 -> 0, of which waited for: 13 -> 0; matrix products, arithmetic and copies ran while one was open for 2% -> 0% of each run, Pallas kernels for 0% -> 0%
where the time goes in v2:
time: 154 us
  Pallas kernels  150 us (97%)
  local copies, waits for them, and re-layouts  2.91 us (2%)
    pallas_call x1, Pallas kernels, on_device(): pl.pallas_call(functools.partial(kernel, sizes), out_shape=jax.ShapeDtype...  150 us

profile of v2, /device:TPU:7, one launch (start us, length us, event | category | flops | bytes accessed | tf_op | source)
XLA Modules:
  0.0 153.8 jit_solution(2370999122138550159)
XLA Ops:
  0.7 1.3 reshape.3.image_in
  2.0 150.2 %shard_map.100 = bf16[128,512]{1,0:T(8,128)(2,1)} custom-call(s32[2]{0:T(128)} %tiles_in.1, s32[2]{0:T(128)} %lengths_in.1, s32[2]{0:T(128)} %pick_in.1, f32[1]{0:T(128)S(6)} %copy.12.gate_in, bf16[128,512]{1,0:T(8,128)(2,1)} %x_in.1, bf16[8,1280]{1,0:T(8,128)(2,1)} %reshape.3.image_in, f32[1,4096]{1,0:T(1,128)} %gain_in.1, bf16[256,512]{1,0:T(8,128)(2,1)} %bitcast.6, ...), custom_call_target="tpu_custom_call" | custom-call | tf_op jit(solution)/shard_map/pallas_call | solution.py:475
  152.2 1.6 %copy.13 = bf16[1,128,512]{2,1,0:T(8,128)(2,1)} copy(bf16[1,128,512]{2,1,0:T(8,128)(2,1)} %bitcast.5) | data formatting | bytes 262144
